TPU v7x, 32 devices: a whole 2x2x4 slice. The times are simulated.
32 devices in a mesh: aux: 4 (over y, x), occ: 8 (over z, core).
Axes of the slice: x: 2, y: 2, z: 4, core: 2. Of those that a mesh axis runs over, the one named last changes fastest.
Arguments:
- three_index: bfloat16 [2048, 32, 256], P('aux', 'occ'), may hold values from -0.8984375 to 0.8984375
- pair_list: int32 [8, 6], replicated, may hold values from 0 to 7
- pair_counts: int32 [8], replicated, may hold values from 1 to 6, as said below
- domains: int32 [8, 256], replicated, may hold values from 0 to 2047
- pao_energy: float32 [2048], replicated, may hold values from 0.5 to 3
- occ_energy: float32 [32], replicated, may hold values from -2 to -0.3
Outputs:
- density: bfloat16 [2048, 32, 256], P('aux', 'occ')
- pair_energy: float32 [8, 6], P('occ')
Inputs may be any that keep to these rules, and one draw needn't show every extreme that they name: `pair_list`: slots at or past a block's count are unused. `pair_counts`: some block uses all 6 slots.
All inputs are finite; a program needn't handle non-finite values.
Results may differ from a plain program's by a relative error of at most 0.0031.
Values may be sent and summed in bfloat16 or wider, within the bound.
No kernel may reach another device: no remote copies, remote signals or barrier semaphores. Data moves between devices by JAX's collectives and lax.ppermute only.
A program may use at most 64 MiB of HBM per device.

v0:
```python
import jax
import jax.numpy as jnp
from jax import lax
from jax.sharding import PartitionSpec as P


def per_device(three_index, pair_list, pair_counts, domains, pao_energy, occ_energy):
    aux_local, occ_dev, dom_width = three_index.shape
    pair_rows = occ_dev * dom_width
    block_count = lax.axis_size("occ")
    block_id = lax.axis_index("occ")
    aux_count = lax.axis_size("aux")
    aux_rank = lax.axis_index("aux")
    share_rows = pair_rows // aux_count
    slot_total = pair_list.shape[1]
    own_block = three_index.reshape(aux_local, pair_rows)
    levels = jnp.take(pao_energy, domains, axis=0)
    occ_levels = occ_energy.reshape(block_count, occ_dev)
    denoms = (levels[:, None, :] - occ_levels[:, :, None]).reshape(block_count, pair_rows)
    own_denom = denoms[block_id]
    row_denom = lax.dynamic_slice_in_dim(own_denom, aux_rank * share_rows, share_rows, 0)
    my_pairs = pair_list[block_id]
    my_count = pair_counts[block_id]
    all_blocks = lax.all_gather(own_block[None], "occ", axis=0, tiled=True)

    def partner_of(slot_id):
        return all_blocks[my_pairs[slot_id]]

    def scaled(integrals, slot_id):
        partner_id = my_pairs[slot_id]
        slot_valid = (slot_id < my_count).astype(jnp.float32)
        amplitude = (
            integrals / (row_denom[:, None] + denoms[partner_id][None, :]) * slot_valid
        ).astype(jnp.bfloat16)
        energy_part = jnp.sum(amplitude.astype(jnp.float32) * integrals) / (pair_rows * pair_rows)
        return (amplitude, energy_part)

    energies = jnp.zeros((slot_total,), jnp.float32)

    def one_slot(slot_id, state_pair):
        density, energies = state_pair
        partner = partner_of(slot_id)
        integrals = lax.psum_scatter(
            jnp.einsum("ar,ac->rc", own_block, partner, preferred_element_type=jnp.float32),
            "aux",
            scatter_dimension=0,
            tiled=True,
        )
        amplitude, energy_part = scaled(integrals, slot_id)
        density = density + jnp.einsum(
            "ac,rc->ar",
            partner,
            lax.all_gather(amplitude, "aux", axis=0, tiled=True),
            preferred_element_type=jnp.float32,
        )
        return (density, energies.at[slot_id].set(energy_part))

    density, energies = lax.fori_loop(
        0, slot_total, one_slot, (jnp.zeros((aux_local, pair_rows), jnp.float32), energies)
    )
    density_out = density.astype(jnp.bfloat16)
    energies = lax.psum(energies, "aux")
    return (density_out.reshape(aux_local, occ_dev, dom_width), energies[None])


def solution(mesh):
    placed = (P("aux", "occ", None), P(), P(), P(), P(), P())
    return jax.shard_map(
        per_device,
        mesh=mesh,
        in_specs=placed,
        out_specs=(P("aux", "occ", None), P("occ", None)),
        check_vma=False,
    )
```

profile of v0, /device:TPU:0, one launch (start us, length us, event | category | flops | bytes accessed | tf_op | source)
XLA Modules:
  0.0 722.3 jit_solution(9689059102581887274)
XLA Ops:
  9.9 11.8 %gather_fusion = f32[2048]{0:T(1024)S(1)} fusion(f32[2048]{0:T(1024)S(1)} %copy-done, s32[2048]{0:T(1024)S(1)} %broadcast_clamp_fusion), kind=kCustom, calls=%fused_computation | custom fusion | bytes 24576 | tf_op jit(solution)/shard_map/jit(_take)/gather | solution.py:17
  24.7 70.3 %all-gather.3.cloned.1.call-done = bf16[8,512,1024]{2,1,0:T(8,128)(2,1)} async-done(((bf16[1,512,1024]{2,1,0:T(8,128)(2,1)}), bf16[8,512,1024]{2,1,0:T(8,128)(2,1)}) %all-gather.3.cloned.1.call-update) | async-done | bytes 8388624 | tf_op jit(solution)/shard_map/all_gather | solution.py:24
  95.0 609.7 %while.17 = (s32[]{:T(128)}, f32[512,1024]{1,0:T(8,128)S(1)}, f32[6]{0:T(128)S(1)}, s32[6]{0:T(128)S(1)}, bf16[8,512,1024]{2,1,0:T(8,128)(2,1)}, /*index=5*/bf16...) while((s32[]{:T(128)}, f32[512,1024]{1,0:T(8,128)S(1)}, ...), condition=%wide.region_3.4_spmd.clone, body=%wide.region_0.3_spmd.clone.sunk | while | flops 2150367232 | bytes 38811020 | solution.py:58
  97.5 4.8 convolution_bitcast_fusion.2
  103.0 50.6 %reduce-scatter.2.cloned.1.call-done = f32[256,1024]{0,1:T(8,128)} async-done(((f32[1024,1024]{0,1:T(8,128)}), f32[256,1024]{0,1:T(8,128)}) %reduce-scatter.2.cloned.1.call-update) | async-done | bytes 1048592 | tf_op jit(solution)/shard_map/while/body/eval_jaxpr/reduce_scatter | solution.py:43
  153.6 3.0 multiply_reduce_fusion.2
  157.4 34.3 %all-gather.5.cloned.1.call-done = bf16[1024,1024]{0,1:T(8,128)(2,1)} async-done(((bf16[256,1024]{0,1:T(8,128)(2,1)}), bf16[1024,1024]{0,1:T(8,128)(2,1)}) %all-gather.5.cloned.1.call-update) | async-done | bytes 2097168 | tf_op jit(solution)/shard_map/while/body/eval_jaxpr/all_gather | solution.py:53
  191.8 3.5 select_add_fusion.2
  197.9 4.8 convolution_bitcast_fusion.2
  203.4 52.1 %reduce-scatter.2.cloned.1.call-done = f32[256,1024]{0,1:T(8,128)} async-done(((f32[1024,1024]{0,1:T(8,128)}), f32[256,1024]{0,1:T(8,128)}) %reduce-scatter.2.cloned.1.call-update) | async-done | bytes 1048592 | tf_op jit(solution)/shard_map/while/body/eval_jaxpr/reduce_scatter | solution.py:43
  255.4 3.0 multiply_reduce_fusion.2
  259.3 34.3 %all-gather.5.cloned.1.call-done = bf16[1024,1024]{0,1:T(8,128)(2,1)} async-done(((bf16[256,1024]{0,1:T(8,128)(2,1)}), bf16[1024,1024]{0,1:T(8,128)(2,1)}) %all-gather.5.cloned.1.call-update) | async-done | bytes 2097168 | tf_op jit(solution)/shard_map/while/body/eval_jaxpr/all_gather | solution.py:53
  293.6 3.5 select_add_fusion.2
  299.7 4.8 convolution_bitcast_fusion.2
  305.2 52.1 %reduce-scatter.2.cloned.1.call-done = f32[256,1024]{0,1:T(8,128)} async-done(((f32[1024,1024]{0,1:T(8,128)}), f32[256,1024]{0,1:T(8,128)}) %reduce-scatter.2.cloned.1.call-update) | async-done | bytes 1048592 | tf_op jit(solution)/shard_map/while/body/eval_jaxpr/reduce_scatter | solution.py:43
  357.3 3.0 multiply_reduce_fusion.2
  361.2 34.3 %all-gather.5.cloned.1.call-done = bf16[1024,1024]{0,1:T(8,128)(2,1)} async-done(((bf16[256,1024]{0,1:T(8,128)(2,1)}), bf16[1024,1024]{0,1:T(8,128)(2,1)}) %all-gather.5.cloned.1.call-update) | async-done | bytes 2097168 | tf_op jit(solution)/shard_map/while/body/eval_jaxpr/all_gather | solution.py:53
  395.5 3.5 select_add_fusion.2
  401.6 4.8 convolution_bitcast_fusion.2
  407.1 52.1 %reduce-scatter.2.cloned.1.call-done = f32[256,1024]{0,1:T(8,128)} async-done(((f32[1024,1024]{0,1:T(8,128)}), f32[256,1024]{0,1:T(8,128)}) %reduce-scatter.2.cloned.1.call-update) | async-done | bytes 1048592 | tf_op jit(solution)/shard_map/while/body/eval_jaxpr/reduce_scatter | solution.py:43
  459.2 3.0 multiply_reduce_fusion.2
  463.0 34.3 %all-gather.5.cloned.1.call-done = bf16[1024,1024]{0,1:T(8,128)(2,1)} async-done(((bf16[256,1024]{0,1:T(8,128)(2,1)}), bf16[1024,1024]{0,1:T(8,128)(2,1)}) %all-gather.5.cloned.1.call-update) | async-done | bytes 2097168 | tf_op jit(solution)/shard_map/while/body/eval_jaxpr/all_gather | solution.py:53
  497.4 3.5 select_add_fusion.2
  503.5 4.8 convolution_bitcast_fusion.2
  509.0 52.1 %reduce-scatter.2.cloned.1.call-done = f32[256,1024]{0,1:T(8,128)} async-done(((f32[1024,1024]{0,1:T(8,128)}), f32[256,1024]{0,1:T(8,128)}) %reduce-scatter.2.cloned.1.call-update) | async-done | bytes 1048592 | tf_op jit(solution)/shard_map/while/body/eval_jaxpr/reduce_scatter | solution.py:43
  564.9 34.3 %all-gather.5.cloned.1.call-done = bf16[1024,1024]{0,1:T(8,128)(2,1)} async-done(((bf16[256,1024]{0,1:T(8,128)(2,1)}), bf16[1024,1024]{0,1:T(8,128)(2,1)}) %all-gather.5.cloned.1.call-update) | async-done | bytes 2097168 | tf_op jit(solution)/shard_map/while/body/eval_jaxpr/all_gather | solution.py:53
  599.2 3.5 select_add_fusion.2
  605.4 4.8 convolution_bitcast_fusion.2
  610.9 52.1 %reduce-scatter.2.cloned.1.call-done = f32[256,1024]{0,1:T(8,128)} async-done(((f32[1024,1024]{0,1:T(8,128)}), f32[256,1024]{0,1:T(8,128)}) %reduce-scatter.2.cloned.1.call-update) | async-done | bytes 1048592 | tf_op jit(solution)/shard_map/while/body/eval_jaxpr/reduce_scatter | solution.py:43
  666.8 34.3 %all-gather.5.cloned.1.call-done = bf16[1024,1024]{0,1:T(8,128)(2,1)} async-done(((bf16[256,1024]{0,1:T(8,128)(2,1)}), bf16[1024,1024]{0,1:T(8,128)(2,1)}) %all-gather.5.cloned.1.call-update) | async-done | bytes 2097168 | tf_op jit(solution)/shard_map/while/body/eval_jaxpr/all_gather | solution.py:53
  701.1 3.5 select_add_fusion.2
  706.4 9.4 %psum.7 = f32[1,6]{1,0:T(1,128)} all-reduce(f32[1,6]{1,0:T(1,128)S(1)} %bitcast.49), channel_id=1, replica_groups=mesh['aux'=4,'occ'=8] {'aux'}, use_global_device_ids=true, to_apply=%region_4.5 | all-reduce | flops 6 | bytes 48 | tf_op jit(solution)/shard_map/psum | solution.py:62
  (73 shorter events, 18.6 us)
Async XLA Ops:
  7.2 2.7 copy-start
  7.2 2.7 copy-start.2
  7.2 87.8 %all-gather.3.cloned.1.call-start = ((), (), s32[]{:S(2)}) async-start(), calls=%async_computation.1 | async-start | bytes 9437184 | tf_op jit(solution)/shard_map/all_gather | solution.py:24
  9.9 11.8 %copy-start.3 = (f32[32]{0:T(128)S(1)}, f32[32]{0:T(128)}, u32[]{:S(2)}) copy-start(f32[32]{0:T(128)} %param.15) | copy-start | bytes 388
  9.9 12.0 %copy-start.4 = (s32[8]{0:T(128)S(1)}, s32[8]{0:T(128)}, u32[]{:S(2)}) copy-start(s32[8]{0:T(128)} %param.12) | copy-start | bytes 100
  9.9 12.6 %copy-start.1 = (bf16[512,4,256]{2,1,0:T(4,128)(2,1)S(1)}, bf16[512,4,256]{2,1,0:T(4,128)(2,1)}, u32[]{:S(2)}) copy-start(bf16[512,4,256]{2,1,0:T(4,128)(2,1)} %param.10) | copy-start | bytes 3145732
  95.0 58.6 %reduce-scatter.2.cloned.1.call-start = ((), (), s32[]{:S(2)}) async-start(), calls=%async_computation.2 | async-start | bytes 5242880 | tf_op jit(solution)/shard_map/while/body/eval_jaxpr/reduce_scatter | solution.py:43
  102.3 89.5 %all-gather.5.cloned.1.call-start = ((), (), s32[]{:S(2)}) async-start(), calls=%async_computation.3 | async-start | bytes 2621440 | tf_op jit(solution)/shard_map/while/body/eval_jaxpr/all_gather | solution.py:53
  195.3 60.1 %reduce-scatter.2.cloned.1.call-start = ((), (), s32[]{:S(2)}) async-start(), calls=%async_computation.2 | async-start | bytes 5242880 | tf_op jit(solution)/shard_map/while/body/eval_jaxpr/reduce_scatter | solution.py:43
  202.7 90.9 %all-gather.5.cloned.1.call-start = ((), (), s32[]{:S(2)}) async-start(), calls=%async_computation.3 | async-start | bytes 2621440 | tf_op jit(solution)/shard_map/while/body/eval_jaxpr/all_gather | solution.py:53
  297.2 60.1 %reduce-scatter.2.cloned.1.call-start = ((), (), s32[]{:S(2)}) async-start(), calls=%async_computation.2 | async-start | bytes 5242880 | tf_op jit(solution)/shard_map/while/body/eval_jaxpr/reduce_scatter | solution.py:43
  304.6 90.9 %all-gather.5.cloned.1.call-start = ((), (), s32[]{:S(2)}) async-start(), calls=%async_computation.3 | async-start | bytes 2621440 | tf_op jit(solution)/shard_map/while/body/eval_jaxpr/all_gather | solution.py:53
  399.0 60.1 %reduce-scatter.2.cloned.1.call-start = ((), (), s32[]{:S(2)}) async-start(), calls=%async_computation.2 | async-start | bytes 5242880 | tf_op jit(solution)/shard_map/while/body/eval_jaxpr/reduce_scatter | solution.py:43
  406.4 90.9 %all-gather.5.cloned.1.call-start = ((), (), s32[]{:S(2)}) async-start(), calls=%async_computation.3 | async-start | bytes 2621440 | tf_op jit(solution)/shard_map/while/body/eval_jaxpr/all_gather | solution.py:53
  500.9 60.1 %reduce-scatter.2.cloned.1.call-start = ((), (), s32[]{:S(2)}) async-start(), calls=%async_computation.2 | async-start | bytes 5242880 | tf_op jit(solution)/shard_map/while/body/eval_jaxpr/reduce_scatter | solution.py:43
  508.3 90.9 %all-gather.5.cloned.1.call-start = ((), (), s32[]{:S(2)}) async-start(), calls=%async_computation.3 | async-start | bytes 2621440 | tf_op jit(solution)/shard_map/while/body/eval_jaxpr/all_gather | solution.py:53
  602.8 60.1 %reduce-scatter.2.cloned.1.call-start = ((), (), s32[]{:S(2)}) async-start(), calls=%async_computation.2 | async-start | bytes 5242880 | tf_op jit(solution)/shard_map/while/body/eval_jaxpr/reduce_scatter | solution.py:43
  610.2 90.9 %all-gather.5.cloned.1.call-start = ((), (), s32[]{:S(2)}) async-start(), calls=%async_computation.3 | async-start | bytes 2621440 | tf_op jit(solution)/shard_map/while/body/eval_jaxpr/all_gather | solution.py:53
Sparse Core Ops, SparseCore 0:
  10.2 84.7 all-gather.2
  102.4 51.0 reduce-scatter.1
  156.7 35.0 all-gather.4
  202.8 52.5 reduce-scatter.1
  258.6 35.0 all-gather.4
  304.7 52.5 reduce-scatter.1
  360.4 35.0 all-gather.4
  406.6 52.5 reduce-scatter.1
  462.3 35.0 all-gather.4
  508.4 52.5 reduce-scatter.1
  564.2 35.0 all-gather.4
  610.3 52.5 reduce-scatter.1
  666.0 35.0 all-gather.4
where the time goes:
time: 723 us; the launch traced here: 722 us
  waiting for transfers between devices  587 us (81%)
  matrix products  49.8 us (7%)
  local copies, waits for them, and re-layouts  22.4 us (3%)
  loops' own time  19.9 us (3%)
  other arithmetic  19.2 us (3%)
  between operations  13.9 us (2%)
  blocking collectives  9.41 us (1%)
    reduce_scatter x6, waiting for transfers between devices, one_slot(): lax.psum_scatter(jnp.einsum('ar,ac->rc', own_block, partner, preferred_el...  311 us
    all_gather x6, waiting for transfers between devices, one_slot(): lax.all_gather(amplitude, 'aux', axis=0, tiled=True)  206 us
    all_gather x1, waiting for transfers between devices, per_device(): all_blocks = lax.all_gather(own_block[None], 'occ', axis=0, tiled=True)  70.3 us
    dot_general x6, matrix products, one_slot(): jnp.einsum('ar,ac->rc', own_block, partner, preferred_element_type=jnp.fl...  28.8 us
    dot_general x6, matrix products, one_slot(): jnp.einsum('ac,rc->ar', partner, lax.all_gather(amplitude, 'aux', axis=0,...  21 us
    another operation x1, loops' own time, per_device(): lax.fori_loop(0, slot_total, one_slot, (jnp.zeros((aux_local, pair_rows),...  19.9 us
    reduce_sum x6, other arithmetic, scaled(): jnp.sum(amplitude.astype(jnp.float32) * integrals) / (pair_rows * pair_rows)  17.9 us
  transfers between devices with their start and end apart: 13, of which 13 were waited for; matrix products, arithmetic and copies ran while one was open for 2% of the time, Pallas kernels for 0%

commit v1 on v0

--- a/solution.py
+++ b/solution.py
@@ -50,7 +50,9 @@
         density = density + jnp.einsum(
             "ac,rc->ar",
             partner,
-            lax.all_gather(amplitude, "aux", axis=0, tiled=True),
+            jnp.concatenate(
+                lax.all_to_all(jnp.stack([amplitude] * lax.axis_size("aux")), "aux", 0, 0), axis=0
+            ),
             preferred_element_type=jnp.float32,
         )
         return (density, energies.at[slot_id].set(energy_part))

time: 723 us -> 696 us (0.963)
  waiting for transfers between devices: 587 us -> 527 us
  starting transfers between devices: 0.51 us -> 21.7 us
  local copies, waits for them, and re-layouts: 22.4 us -> 32.3 us
    all_gather x6 -> x0, waiting for transfers between devices: 206 us -> none  [one_slot(): lax.all_gather(amplitude, 'aux', axis=0, tiled=True)]
    all_to_all x0 -> x6, waiting for transfers between devices: none -> 145 us  [one_slot(): lax.all_to_all(jnp.stack([amplitude] * lax.axis_size('aux')), 'aux', 0, 0)]
    all_to_all x0 -> x6, starting transfers between devices: none -> 21.6 us  [one_slot(): lax.all_to_all(jnp.stack([amplitude] * lax.axis_size('aux')), 'aux', 0, 0)]
    another operation x1 -> x7, local copies, waits for them, and re-layouts: 0.01 us -> 9.72 us  [the longest x6 9.72 us: one_slot(): jnp.stack([amplitude] * lax.axis_size('aux'))]
where the time goes in v1:
time: 696 us; the launch traced here: 694 us
  waiting for transfers between devices  527 us (76%)
  matrix products  53.5 us (8%)
  local copies, waits for them, and re-layouts  32.3 us (5%)
  starting transfers between devices  21.7 us (3%)
  loops' own time  20 us (3%)
  other arithmetic  16.4 us (2%)
  between operations  14.2 us (2%)
  blocking collectives  9.36 us (1%)
    reduce_scatter x6, waiting for transfers between devices, one_slot(): lax.psum_scatter(jnp.einsum('ar,ac->rc', own_block, partner, preferred_el...  311 us
    all_to_all x6, waiting for transfers between devices, one_slot(): lax.all_to_all(jnp.stack([amplitude] * lax.axis_size('aux')), 'aux', 0, 0)  145 us
    all_gather x1, waiting for transfers between devices, per_device(): all_blocks = lax.all_gather(own_block[None], 'occ', axis=0, tiled=True)  71.3 us
    dot_general x6, matrix products, one_slot(): jnp.einsum('ar,ac->rc', own_block, partner, preferred_element_type=jnp.fl...  27 us
    dot_general x6, matrix products, one_slot(): jnp.einsum('ac,rc->ar', partner, jnp.concatenate(lax.all_to_all(jnp.stack...  26.6 us
    all_to_all x6, starting transfers between devices, one_slot(): lax.all_to_all(jnp.stack([amplitude] * lax.axis_size('aux')), 'aux', 0, 0)  21.6 us
    another operation x1, loops' own time, per_device(): lax.fori_loop(0, slot_total, one_slot, (jnp.zeros((aux_local, pair_rows),...  20 us
  transfers between devices with their start and end apart: 13, of which 13 were waited for; matrix products, arithmetic and copies ran while one was open for 2% of the time, Pallas kernels for 0%

profile of v1, /device:TPU:0, one launch (start us, length us, event | category | flops | bytes accessed | tf_op | source)
XLA Modules:
  0.0 694.3 jit_solution(16731162109898205058)
XLA Ops:
  9.9 11.8 %gather_fusion = f32[2048]{0:T(1024)S(1)} fusion(f32[2048]{0:T(1024)S(1)} %copy-done, s32[2048]{0:T(1024)S(1)} %broadcast_clamp_fusion), kind=kCustom, calls=%fused_computation | custom fusion | bytes 24576 | tf_op jit(solution)/shard_map/jit(_take)/gather | solution.py:17
  23.7 71.3 %all-gather.2.cloned.1.call-done = bf16[8,512,1024]{2,1,0:T(8,128)(2,1)} async-done(((bf16[1,512,1024]{2,1,0:T(8,128)(2,1)}), bf16[8,512,1024]{2,1,0:T(8,128)(2,1)}) %all-gather.2.cloned.1.call-update) | async-done | bytes 8388624 | tf_op jit(solution)/shard_map/all_gather | solution.py:24
  95.0 579.8 %while.17 = (s32[]{:T(128)}, f32[512,1024]{1,0:T(8,128)}, f32[6]{0:T(128)S(1)}, s32[6]{0:T(128)S(1)}, bf16[8,512,1024]{2,1,0:T(8,128)(2,1)}, /*index=5*/bf16[512...) while((s32[]{:T(128)}, f32[512,1024]{1,0:T(8,128)}, ...), condition=%wide.region_3.4_spmd.clone, body=%wide.region_0.3_spmd.clone.sunk | while | flops 2150367232 | bytes 40908164 | solution.py:60
  97.5 4.5 convolution_bitcast_fusion.2
  102.7 50.5 %reduce-scatter.2.cloned.1.call-done = f32[256,1024]{0,1:T(8,128)} async-done(((f32[1024,1024]{0,1:T(8,128)}), f32[256,1024]{0,1:T(8,128)}) %reduce-scatter.2.cloned.1.call-update) | async-done | bytes 1048592 | tf_op jit(solution)/shard_map/while/body/eval_jaxpr/reduce_scatter | solution.py:43
  157.4 3.6 all-to-all-start
  161.8 24.1 %all-to-all-done = bf16[4,256,1024]{2,1,0:T(8,128)(2,1)S(1)} async-done(((bf16[4,256,1024]{2,1,0:T(8,128)(2,1)}), bf16[4,256,1024]{2,1,0:T(8,128)(2,1)S(1)}, u32[]{:S(2)}, u32[]{:S(2)}) %all-to-all-start) | async-done | bytes 2097184 | tf_op jit(solution)/shard_map/while/body/eval_jaxpr/all_to_all | solution.py:54
  185.9 3.8 select_add_fusion.2
  192.3 4.5 convolution_bitcast_fusion.2
  197.5 52.1 %reduce-scatter.2.cloned.1.call-done = f32[256,1024]{0,1:T(8,128)} async-done(((f32[1024,1024]{0,1:T(8,128)}), f32[256,1024]{0,1:T(8,128)}) %reduce-scatter.2.cloned.1.call-update) | async-done | bytes 1048592 | tf_op jit(solution)/shard_map/while/body/eval_jaxpr/reduce_scatter | solution.py:43
  253.7 3.6 all-to-all-start
  258.1 24.1 %all-to-all-done = bf16[4,256,1024]{2,1,0:T(8,128)(2,1)S(1)} async-done(((bf16[4,256,1024]{2,1,0:T(8,128)(2,1)}), bf16[4,256,1024]{2,1,0:T(8,128)(2,1)S(1)}, u32[]{:S(2)}, u32[]{:S(2)}) %all-to-all-start) | async-done | bytes 2097184 | tf_op jit(solution)/shard_map/while/body/eval_jaxpr/all_to_all | solution.py:54
  282.2 4.5 select_add_fusion.2
  289.3 4.5 convolution_bitcast_fusion.2
  294.5 52.1 %reduce-scatter.2.cloned.1.call-done = f32[256,1024]{0,1:T(8,128)} async-done(((f32[1024,1024]{0,1:T(8,128)}), f32[256,1024]{0,1:T(8,128)}) %reduce-scatter.2.cloned.1.call-update) | async-done | bytes 1048592 | tf_op jit(solution)/shard_map/while/body/eval_jaxpr/reduce_scatter | solution.py:43
  350.7 3.6 all-to-all-start
  355.1 24.1 %all-to-all-done = bf16[4,256,1024]{2,1,0:T(8,128)(2,1)S(1)} async-done(((bf16[4,256,1024]{2,1,0:T(8,128)(2,1)}), bf16[4,256,1024]{2,1,0:T(8,128)(2,1)S(1)}, u32[]{:S(2)}, u32[]{:S(2)}) %all-to-all-start) | async-done | bytes 2097184 | tf_op jit(solution)/shard_map/while/body/eval_jaxpr/all_to_all | solution.py:54
  379.2 4.5 select_add_fusion.2
  386.3 4.5 convolution_bitcast_fusion.2
  391.5 52.1 %reduce-scatter.2.cloned.1.call-done = f32[256,1024]{0,1:T(8,128)} async-done(((f32[1024,1024]{0,1:T(8,128)}), f32[256,1024]{0,1:T(8,128)}) %reduce-scatter.2.cloned.1.call-update) | async-done | bytes 1048592 | tf_op jit(solution)/shard_map/while/body/eval_jaxpr/reduce_scatter | solution.py:43
  447.6 3.6 all-to-all-start
  452.1 24.1 %all-to-all-done = bf16[4,256,1024]{2,1,0:T(8,128)(2,1)S(1)} async-done(((bf16[4,256,1024]{2,1,0:T(8,128)(2,1)}), bf16[4,256,1024]{2,1,0:T(8,128)(2,1)S(1)}, u32[]{:S(2)}, u32[]{:S(2)}) %all-to-all-start) | async-done | bytes 2097184 | tf_op jit(solution)/shard_map/while/body/eval_jaxpr/all_to_all | solution.py:54
  476.2 4.5 select_add_fusion.2
  483.3 4.5 convolution_bitcast_fusion.2
  488.5 52.0 %reduce-scatter.2.cloned.1.call-done = f32[256,1024]{0,1:T(8,128)} async-done(((f32[1024,1024]{0,1:T(8,128)}), f32[256,1024]{0,1:T(8,128)}) %reduce-scatter.2.cloned.1.call-update) | async-done | bytes 1048592 | tf_op jit(solution)/shard_map/while/body/eval_jaxpr/reduce_scatter | solution.py:43
  549.1 24.1 %all-to-all-done = bf16[4,256,1024]{2,1,0:T(8,128)(2,1)S(1)} async-done(((bf16[4,256,1024]{2,1,0:T(8,128)(2,1)}), bf16[4,256,1024]{2,1,0:T(8,128)(2,1)S(1)}, u32[]{:S(2)}, u32[]{:S(2)}) %all-to-all-start) | async-done | bytes 2097184 | tf_op jit(solution)/shard_map/while/body/eval_jaxpr/all_to_all | solution.py:54
  573.2 4.5 select_add_fusion.2
  580.2 4.5 convolution_bitcast_fusion.2
  585.5 52.1 %reduce-scatter.2.cloned.1.call-done = f32[256,1024]{0,1:T(8,128)} async-done(((f32[1024,1024]{0,1:T(8,128)}), f32[256,1024]{0,1:T(8,128)}) %reduce-scatter.2.cloned.1.call-update) | async-done | bytes 1048592 | tf_op jit(solution)/shard_map/while/body/eval_jaxpr/reduce_scatter | solution.py:43
  646.1 24.1 %all-to-all-done = bf16[4,256,1024]{2,1,0:T(8,128)(2,1)S(1)} async-done(((bf16[4,256,1024]{2,1,0:T(8,128)(2,1)}), bf16[4,256,1024]{2,1,0:T(8,128)(2,1)S(1)}, u32[]{:S(2)}, u32[]{:S(2)}) %all-to-all-start) | async-done | bytes 2097184 | tf_op jit(solution)/shard_map/while/body/eval_jaxpr/all_to_all | solution.py:54
  670.2 4.5 select_add_fusion.2
  678.1 9.4 %psum.7 = f32[1,6]{1,0:T(1,128)} all-reduce(f32[1,6]{1,0:T(1,128)S(1)} %bitcast.53), channel_id=1, replica_groups=mesh['aux'=4,'occ'=8] {'aux'}, use_global_device_ids=true, to_apply=%region_4.5 | all-reduce | flops 6 | bytes 48 | tf_op jit(solution)/shard_map/psum | solution.py:64
  (79 shorter events, 44.3 us)
Async XLA Ops:
  7.2 2.7 copy-start
  7.2 2.7 copy-start.2
  7.2 87.8 %all-gather.2.cloned.1.call-start = ((), (), s32[]{:S(2)}) async-start(), calls=%async_computation.2 | async-start | bytes 9437184 | tf_op jit(solution)/shard_map/all_gather | solution.py:24
  9.9 11.8 %copy-start.3 = (f32[32]{0:T(128)S(1)}, f32[32]{0:T(128)}, u32[]{:S(2)}) copy-start(f32[32]{0:T(128)} %param.15) | copy-start | bytes 388
  9.9 12.0 %copy-start.4 = (s32[8]{0:T(128)S(1)}, s32[8]{0:T(128)}, u32[]{:S(2)}) copy-start(s32[8]{0:T(128)} %param.12) | copy-start | bytes 100
  9.9 12.7 %copy-start.1 = (bf16[512,4,256]{2,1,0:T(4,128)(2,1)S(1)}, bf16[512,4,256]{2,1,0:T(4,128)(2,1)}, u32[]{:S(2)}) copy-start(bf16[512,4,256]{2,1,0:T(4,128)(2,1)} %param.10) | copy-start | bytes 3145732
  95.0 58.3 %reduce-scatter.2.cloned.1.call-start = ((), (), s32[]{:S(2)}) async-start(), calls=%async_computation.3 | async-start | bytes 5242880 | tf_op jit(solution)/shard_map/while/body/eval_jaxpr/reduce_scatter | solution.py:43
  157.4 28.6 %all-to-all-start = ((bf16[4,256,1024]{2,1,0:T(8,128)(2,1)}), bf16[4,256,1024]{2,1,0:T(8,128)(2,1)S(1)}, u32[]{:S(2)}, u32[]{:S(2)}) async-start(bf16[4,256,1024]{2,1,0:T(8,128)(2,1)} %stack.13), calls=%async_computation.1 | async-start | bytes 4194304 | tf_op jit(solution)/shard_map/while/body/eval_jaxpr/all_to_all | solution.py:54
  189.8 59.8 %reduce-scatter.2.cloned.1.call-start = ((), (), s32[]{:S(2)}) async-start(), calls=%async_computation.3 | async-start | bytes 5242880 | tf_op jit(solution)/shard_map/while/body/eval_jaxpr/reduce_scatter | solution.py:43
  253.7 28.6 %all-to-all-start = ((bf16[4,256,1024]{2,1,0:T(8,128)(2,1)}), bf16[4,256,1024]{2,1,0:T(8,128)(2,1)S(1)}, u32[]{:S(2)}, u32[]{:S(2)}) async-start(bf16[4,256,1024]{2,1,0:T(8,128)(2,1)} %stack.13), calls=%async_computation.1 | async-start | bytes 4194304 | tf_op jit(solution)/shard_map/while/body/eval_jaxpr/all_to_all | solution.py:54
  286.8 59.8 %reduce-scatter.2.cloned.1.call-start = ((), (), s32[]{:S(2)}) async-start(), calls=%async_computation.3 | async-start | bytes 5242880 | tf_op jit(solution)/shard_map/while/body/eval_jaxpr/reduce_scatter | solution.py:43
  350.7 28.5 %all-to-all-start = ((bf16[4,256,1024]{2,1,0:T(8,128)(2,1)}), bf16[4,256,1024]{2,1,0:T(8,128)(2,1)S(1)}, u32[]{:S(2)}, u32[]{:S(2)}) async-start(bf16[4,256,1024]{2,1,0:T(8,128)(2,1)} %stack.13), calls=%async_computation.1 | async-start | bytes 4194304 | tf_op jit(solution)/shard_map/while/body/eval_jaxpr/all_to_all | solution.py:54
  383.7 59.8 %reduce-scatter.2.cloned.1.call-start = ((), (), s32[]{:S(2)}) async-start(), calls=%async_computation.3 | async-start | bytes 5242880 | tf_op jit(solution)/shard_map/while/body/eval_jaxpr/reduce_scatter | solution.py:43
  447.6 28.6 %all-to-all-start = ((bf16[4,256,1024]{2,1,0:T(8,128)(2,1)}), bf16[4,256,1024]{2,1,0:T(8,128)(2,1)S(1)}, u32[]{:S(2)}, u32[]{:S(2)}) async-start(bf16[4,256,1024]{2,1,0:T(8,128)(2,1)} %stack.13), calls=%async_computation.1 | async-start | bytes 4194304 | tf_op jit(solution)/shard_map/while/body/eval_jaxpr/all_to_all | solution.py:54
  480.8 59.8 %reduce-scatter.2.cloned.1.call-start = ((), (), s32[]{:S(2)}) async-start(), calls=%async_computation.3 | async-start | bytes 5242880 | tf_op jit(solution)/shard_map/while/body/eval_jaxpr/reduce_scatter | solution.py:43
  544.6 28.5 %all-to-all-start = ((bf16[4,256,1024]{2,1,0:T(8,128)(2,1)}), bf16[4,256,1024]{2,1,0:T(8,128)(2,1)S(1)}, u32[]{:S(2)}, u32[]{:S(2)}) async-start(bf16[4,256,1024]{2,1,0:T(8,128)(2,1)} %stack.13), calls=%async_computation.1 | async-start | bytes 4194304 | tf_op jit(solution)/shard_map/while/body/eval_jaxpr/all_to_all | solution.py:54
  577.7 59.8 %reduce-scatter.2.cloned.1.call-start = ((), (), s32[]{:S(2)}) async-start(), calls=%async_computation.3 | async-start | bytes 5242880 | tf_op jit(solution)/shard_map/while/body/eval_jaxpr/reduce_scatter | solution.py:43
  641.6 28.6 %all-to-all-start = ((bf16[4,256,1024]{2,1,0:T(8,128)(2,1)}), bf16[4,256,1024]{2,1,0:T(8,128)(2,1)S(1)}, u32[]{:S(2)}, u32[]{:S(2)}) async-start(bf16[4,256,1024]{2,1,0:T(8,128)(2,1)} %stack.13), calls=%async_computation.1 | async-start | bytes 4194304 | tf_op jit(solution)/shard_map/while/body/eval_jaxpr/all_to_all | solution.py:54
Sparse Core Ops, SparseCore 0:
  10.2 84.7 all-gather.1
  102.1 51.0 reduce-scatter.1
  196.9 52.5 reduce-scatter.1
  293.9 52.5 reduce-scatter.1
  390.9 52.5 reduce-scatter.1
  487.9 52.5 reduce-scatter.1
  584.9 52.5 reduce-scatter.1
